TPU v7x, 128 devices: a whole 4x4x4 slice. The times are simulated.
128 devices in a mesh: batch: 4 (over y), seq: 32 (over z, x, core).
Axes of the slice: x: 4, y: 4, z: 4, core: 2. Of those that a mesh axis runs over, the one named last changes fastest.
Arguments:
- queries: bfloat16 [4, 8192, 1024], P('batch', 'seq'), may hold values from -6 to 6
- key_states: bfloat16 [4, 8192, 1024], P('batch', 'seq'), may hold values from -6 to 6
- value_states: bfloat16 [4, 8192, 1024], P('batch', 'seq'), may hold values from -6 to 6
- out_grad: bfloat16 [4, 8192, 1024], P('batch', 'seq'), may hold values from -6 to 6
- memory: float32 [1024, 1024], replicated, may hold values from -6 to 6
- near_device: int32 [64, 8], replicated, may hold values from 0 to 31, all different within a row; in each aligned block of 2 rows (0 to 1, 2 to 3, ...) no two rows name the same one
- near_slot: int32 [64, 8], replicated, may hold values from 0 to 1
- near_count: int32 [64], replicated, may hold values from 1 to 8, 288 in all
- writer_block: int32 [1024], replicated, may hold values from 0 to 63, as said below
Outputs:
- attended: bfloat16 [4, 8192, 1024], P('batch', 'seq')
- query_grad: bfloat16 [4, 8192, 1024], P('batch', 'seq')
- key_grad: bfloat16 [4, 8192, 1024], P('batch', 'seq')
- value_grad: bfloat16 [4, 8192, 1024], P('batch', 'seq')
- memory_grad: float32 [1024, 1024], P('seq')
Inputs may be any that keep to these rules, and one draw needn't show every extreme that they name: Row n of near_device belongs to block n; one row names different indices; the rows of the 2 blocks of one index of seq name no index more than 1 times. writer_block[r] // 2 == r // 32: a memory row is written by a block of the index of seq that holds the row.
All inputs are finite; a program needn't handle non-finite values.
Results may differ from a plain program's by a relative error of at most 0.025.
Values may be sent and summed in bfloat16 or wider, within the bound.
No kernel may reach another device: no remote copies, remote signals or barrier semaphores. Data moves between devices by JAX's collectives and lax.ppermute only.
A program may use at most 192 MiB of HBM per device.

v0:
```python
import math

import jax
import jax.numpy as jnp
from jax import lax
from jax.experimental import pallas as pl
from jax.experimental.pallas import tpu as pltpu
from jax.sharding import PartitionSpec as P

HEADS = 8
HD = 128
BLK = 128
MEM = 1024
NEAR = 8


def _rows_of(col):
    eye = lax.broadcasted_iota(jnp.int32, (BLK, BLK), 0) == lax.broadcasted_iota(jnp.int32, (BLK, BLK), 1)
    return jnp.sum(jnp.where(eye, col, 0.0), axis=0, keepdims=True)


def _query_body(cnt_ref, nb_ref, q_ref, do_ref, mk_ref, *rest):
    k_refs = rest[:NEAR]
    v_refs = rest[NEAR : 2 * NEAR]
    o_ref, dq_ref, tm_ref, st_ref = rest[2 * NEAR :]
    n = pl.program_id(0)
    h = pl.program_id(1)
    heads = pl.num_programs(1)
    scale = 1.0 / math.sqrt(HD)
    f32 = jnp.float32
    nt = (((1,), (1,)), ((), ()))
    tn = (((0,), (0,)), ((), ()))
    q = q_ref[...]
    do = do_ref[...]
    mk = mk_ref[...]
    nk = jnp.concatenate([r[...] for r in k_refs], axis=0)
    nv = jnp.concatenate([r[...] for r in v_refs], axis=0)
    sm = lax.dot_general(q, mk, nt, preferred_element_type=f32) * scale
    sn = lax.dot_general(q, nk, nt, preferred_element_type=f32) * scale
    col = lax.broadcasted_iota(jnp.int32, sn.shape, 1) // BLK
    sn = jnp.where(col < cnt_ref[n], sn, -jnp.inf)
    m = jnp.maximum(jnp.max(sm, axis=1, keepdims=True), jnp.max(sn, axis=1, keepdims=True))
    em = jnp.exp(sm - m)
    en = jnp.exp(sn - m)
    total = jnp.sum(em, axis=1, keepdims=True) + jnp.sum(en, axis=1, keepdims=True)
    pm = em / total
    pn = en / total
    wm = pm.astype(jnp.bfloat16)
    wn = pn.astype(jnp.bfloat16)
    o = (
        jnp.dot(wm, mk, preferred_element_type=f32) + jnp.dot(wn, nv, preferred_element_type=f32)
    ).astype(jnp.bfloat16)
    o_ref[...] = o
    gd = jnp.sum(do.astype(f32) * o.astype(f32), axis=1, keepdims=True)
    dpm = lax.dot_general(do, mk, nt, preferred_element_type=f32)
    dpn = lax.dot_general(do, nv, nt, preferred_element_type=f32)
    dsm = (pm * (dpm - gd)).astype(jnp.bfloat16)
    dsn = (pn * (dpn - gd)).astype(jnp.bfloat16)
    dq_ref[...] = (
        (jnp.dot(dsm, mk, preferred_element_type=f32) + jnp.dot(dsn, nk, preferred_element_type=f32))
        * scale
    ).astype(jnp.bfloat16)
    tm_ref[0] = lax.dot_general(dsm, q, tn, preferred_element_type=f32) * scale + lax.dot_general(
        wm, do, tn, preferred_element_type=f32
    )
    st_ref[pl.ds(h, 1), :] = _rows_of(m)
    st_ref[pl.ds(heads + h, 1), :] = _rows_of(total)
    st_ref[pl.ds(2 * heads + h, 1), :] = _rows_of(gd)


def query_core(counts, near_rows, q, do, mk, kv_all):
    tokens, width = q.shape
    blocks = tokens // BLK
    mem = mk.shape[0]
    heads = width // HD
    nrows = NEAR * BLK
    qspec = pl.BlockSpec((BLK, HD), lambda n, h, c, t: (n, h))
    mspec = pl.BlockSpec((mem, HD), lambda n, h, c, t: (0, h))

    def kv_spec(j, which):
        return pl.BlockSpec((BLK, HD), lambda n, h, c, t: (t[n * NEAR + j], which * heads + h))

    flops = 2 * tokens * width * (mem + nrows) * 4 + 2 * tokens * width * (nrows + mem * 2)
    grid_spec = pltpu.PrefetchScalarGridSpec(
        num_scalar_prefetch=2,
        grid=(blocks, heads),
        in_specs=[qspec, qspec, mspec]
        + [kv_spec(j, 0) for j in range(NEAR)]
        + [kv_spec(j, 1) for j in range(NEAR)],
        out_specs=[
            qspec,
            qspec,
            pl.BlockSpec((1, mem, HD), lambda n, h, c, t: (n, 0, h)),
            pl.BlockSpec((3 * heads, BLK), lambda n, h, c, t: (0, n)),
        ],
    )
    return pl.pallas_call(
        _query_body,
        grid_spec=grid_spec,
        out_shape=[
            jax.ShapeDtypeStruct((tokens, width), jnp.bfloat16),
            jax.ShapeDtypeStruct((tokens, width), jnp.bfloat16),
            jax.ShapeDtypeStruct((blocks, mem, width), jnp.float32),
            jax.ShapeDtypeStruct((3 * heads, tokens), jnp.float32),
        ],
        compiler_params=pltpu.CompilerParams(dimension_semantics=("arbitrary", "arbitrary")),
        cost_estimate=pl.CostEstimate(
            flops=flops,
            transcendentals=tokens * heads * (mem + nrows),
            bytes_accessed=2 * (4 * tokens * width + blocks * mem * width + 2 * blocks * nrows * width)
            + 4 * blocks * mem * width,
        ),
    )(counts, near_rows, q, do, mk, *([kv_all] * (2 * NEAR)))


def _owner_body(src_blk, src_dev, src_slot, src_live, my_slot, qd_ref, st_ref, k_ref, v_ref, dk_ref, dv_ref):
    s = pl.program_id(0)
    heads = k_ref.shape[1] // HD
    scale = 1.0 / math.sqrt(HD)
    f32 = jnp.float32
    nt = (((1,), (1,)), ((), ()))

    @pl.when(s == 0)
    def _():
        dk_ref[...] = jnp.zeros(dk_ref.shape, f32)
        dv_ref[...] = jnp.zeros(dv_ref.shape, f32)

    @pl.when(src_live[s] != 0)
    def _():
        rows = pl.ds(pl.multiple_of(my_slot[s] * BLK, BLK), BLK)
        st = st_ref[0]
        for h in range(heads):
            cols = pl.ds(h * HD, HD)
            q_h = qd_ref[:, cols]
            do_h = qd_ref[:, pl.ds((heads + h) * HD, HD)]
            k_h = k_ref[rows, cols]
            v_h = v_ref[rows, cols]
            row_max = st[h : h + 1]
            row_total = st[heads + h : heads + h + 1]
            grad_dot = st[2 * heads + h : 2 * heads + h + 1]
            score_t = lax.dot_general(k_h, q_h, nt, preferred_element_type=f32) * scale
            prob_t = jnp.exp(score_t - row_max) / row_total
            weight_t = prob_t.astype(jnp.bfloat16)
            dprob_t = lax.dot_general(v_h, do_h, nt, preferred_element_type=f32)
            dscore_t = (prob_t * (dprob_t - grad_dot)).astype(jnp.bfloat16)
            dk = (jnp.dot(dscore_t, q_h, preferred_element_type=f32) * scale).astype(jnp.bfloat16)
            dv = jnp.dot(weight_t, do_h, preferred_element_type=f32).astype(jnp.bfloat16)
            dk_ref[rows, cols] += dk.astype(f32)
            dv_ref[rows, cols] += dv.astype(f32)


def owner_core(src_blk, src_dev, src_slot, src_live, my_slot, qd_all, stats_all, k_loc, v_loc):
    sources = src_blk.shape[0]
    tokens, width = k_loc.shape
    full = pl.BlockSpec((tokens, width), lambda s, a, e, b, c, d: (0, 0))
    grid_spec = pltpu.PrefetchScalarGridSpec(
        num_scalar_prefetch=5,
        grid=(sources,),
        in_specs=[
            pl.BlockSpec((BLK, 2 * width), lambda s, a, e, b, c, d: (a[s], 0)),
            pl.BlockSpec((1, stats_all.shape[1], BLK), lambda s, a, e, b, c, d: (e[s], 0, b[s])),
            full,
            full,
        ],
        out_specs=[full, full],
    )
    return pl.pallas_call(
        _owner_body,
        grid_spec=grid_spec,
        out_shape=[
            jax.ShapeDtypeStruct((tokens, width), jnp.float32),
            jax.ShapeDtypeStruct((tokens, width), jnp.float32),
        ],
        compiler_params=pltpu.CompilerParams(dimension_semantics=("arbitrary",)),
        cost_estimate=pl.CostEstimate(
            flops=sources * 8 * BLK * BLK * width,
            transcendentals=sources * BLK * BLK * (width // HD),
            bytes_accessed=sources * BLK * 2 * width * 2 + 2 * tokens * width * (2 + 8),
        ),
    )(src_blk, src_dev, src_slot, src_live, my_slot, qd_all, stats_all, k_loc, v_loc)


def shards(
    queries,
    key_states,
    value_states,
    out_grad,
    memory,
    near_device,
    near_slot,
    near_count,
    writer_block,
):
    seq_devices = lax.axis_size("seq")
    batch_devices = lax.axis_size("batch")
    my_index = lax.axis_index("seq")
    tokens = queries.shape[1]
    row_width = queries.shape[2]
    local_blocks = tokens // BLK
    rows_dev = MEM // seq_devices
    block_scale = 1.0 / math.sqrt(BLK)
    value_blocks = value_states[0].reshape(local_blocks, BLK, row_width)

    kv_all = lax.all_gather(
        jnp.concatenate([key_states[0], value_states[0]], axis=-1), "seq", axis=0, tiled=True
    )

    value_sums = jnp.sum(value_blocks, axis=1, dtype=jnp.float32)
    all_sums = lax.all_to_all(
        jnp.broadcast_to(value_sums[None], (seq_devices, local_blocks, row_width)),
        "seq",
        split_axis=0,
        concat_axis=0,
        tiled=True,
    ).reshape(seq_devices * local_blocks, row_width)
    memory_keys = (memory + jnp.take(all_sums, writer_block, axis=0) * block_scale).astype(
        jnp.bfloat16
    )
    near_block = (near_device * local_blocks + near_slot).astype(jnp.int32)
    my_near = lax.dynamic_slice_in_dim(near_block, my_index * local_blocks, local_blocks, 0).reshape(-1)
    my_count = lax.dynamic_slice_in_dim(near_count, my_index * local_blocks, local_blocks, 0)
    qd_all = lax.all_gather(
        jnp.concatenate([queries[0], out_grad[0]], axis=-1), "seq", axis=0, tiled=True
    )
    attended_rows, query_rows_grad, term, stats = query_core(
        my_count, my_near, queries[0], out_grad[0], memory_keys, kv_all
    )
    stats_all = lax.all_to_all(
        jnp.broadcast_to(stats[None], (seq_devices,) + stats.shape),
        "seq",
        split_axis=0,
        concat_axis=0,
        tiled=True,
    )
    term_rows, qd_all = lax.optimization_barrier((jnp.sum(term, axis=0).astype(jnp.bfloat16), qd_all))
    row_parts = lax.all_to_all(
        term_rows.reshape(seq_devices, rows_dev, row_width),
        "seq",
        split_axis=0,
        concat_axis=0,
        tiled=True,
    )
    row_grads = jnp.sum(row_parts.astype(jnp.float32), axis=0)
    near_width = near_device.shape[1]
    entries = local_blocks * near_width
    target = near_device.reshape(seq_devices, entries)
    source_slot = near_slot.reshape(seq_devices, entries)
    live = (
        jnp.arange(near_width)[None, None, :]
        < near_count.reshape(seq_devices, local_blocks)[:, :, None]
    ).reshape(seq_devices, entries)
    names_me = target == my_index
    entry_at = jnp.argmax(names_me, axis=1).astype(jnp.int32)
    src_slot = entry_at // near_width
    src_blk = (jnp.arange(seq_devices, dtype=jnp.int32) * local_blocks + src_slot).astype(jnp.int32)
    src_live = jnp.any(names_me & live, axis=1).astype(jnp.int32)
    my_slot = jnp.sum(jnp.where(names_me, source_slot, 0), axis=1).astype(jnp.int32)
    order = jnp.argsort(1 - src_live, stable=True).astype(jnp.int32)
    live_count = jnp.sum(src_live)
    position = jnp.arange(seq_devices, dtype=jnp.int32)
    pick = jnp.where(position < live_count, order, order[jnp.maximum(live_count - 1, 0)])
    live_in_order = (position < live_count).astype(jnp.int32)
    my_writers = (
        lax.dynamic_slice_in_dim(writer_block, my_index * rows_dev, rows_dev, 0)
        - my_index * local_blocks
    )
    writer_match = (my_writers[:, None] == jnp.arange(local_blocks)[None, :])[:, :, None]
    spread = jnp.sum(jnp.where(writer_match, row_grads[:, None, :], 0.0), axis=0) * block_scale
    all_rows = lax.all_to_all(
        jnp.broadcast_to(row_grads[None], (batch_devices, rows_dev, row_width)),
        "batch",
        split_axis=0,
        concat_axis=0,
        tiled=True,
    )
    memory_grad = jnp.sum(all_rows, axis=0)
    dk_sum, dv_sum = owner_core(
        src_blk[pick], pick, src_slot[pick], live_in_order, my_slot[pick], qd_all, stats_all,
        key_states[0], value_states[0],
    )
    value_sum = dv_sum.reshape(local_blocks, BLK, row_width)
    attended = attended_rows.reshape(1, tokens, row_width)
    query_grad = query_rows_grad.reshape(1, tokens, row_width)
    key_grad = dk_sum.astype(jnp.bfloat16).reshape(1, tokens, row_width)
    value_grad = (value_sum + spread[:, None, :]).astype(jnp.bfloat16).reshape(1, tokens, row_width)
    return (attended, query_grad, key_grad, value_grad, memory_grad)


def solution(mesh):
    placed = (
        P("batch", "seq", None),
        P("batch", "seq", None),
        P("batch", "seq", None),
        P("batch", "seq", None),
        P(),
        P(),
        P(),
        P(),
        P(),
    )
    return jax.shard_map(
        shards,
        mesh=mesh,
        in_specs=placed,
        out_specs=(
            P("batch", "seq", None),
            P("batch", "seq", None),
            P("batch", "seq", None),
            P("batch", "seq", None),
            P("seq", None),
        ),
        check_vma=False,
    )
```

profile of v0, /device:TPU:0, one launch (start us, length us, event | category | flops | bytes accessed | tf_op | source)
XLA Modules:
  0.0 317.3 jit_solution(1258434518024504553)
XLA Ops:
  7.2 0.0 all-gather.3.cloned.1.call-start
  7.3 2.3 pad_maximum_fusion
  9.6 0.0 all-gather.5.cloned.1.call-start
  9.7 2.3 pad_maximum_fusion.1
  12.0 0.1 convert_reduce_fusion.1
  12.1 0.8 broadcast_in_dim.70
  12.9 8.3 %all-to-all-start = ((f32[32,2,1024]{2,1,0:T(2,128)}), f32[32,2,1024]{2,1,0:T(2,128)S(1)}, u32[]{:S(2)}, u32[]{:S(2)}) async-start(f32[32,2,1024]{2,1,0:T(2,128)} %broadcast_in_dim.70), calls=%async_computation | async-start | bytes 524288 | tf_op jit(solution)/shard_map/all_to_all | solution.py:209
  21.2 1.2 select_reduce_fusion.1
  22.4 0.1 constant_dynamic-slice_fusion
  22.4 0.1 copy.17
  22.5 0.7 reshape.88.nb_ref
  23.2 0.6 dynamic_slice.12.cnt_ref
  23.8 6.2 %all-to-all-done = f32[32,2,1024]{2,1,0:T(2,128)S(1)} async-done(((f32[32,2,1024]{2,1,0:T(2,128)}), f32[32,2,1024]{2,1,0:T(2,128)S(1)}, u32[]{:S(2)}, u32[]{:S(2)}) %all-to-all-start) | async-done | bytes 262176 | tf_op jit(solution)/shard_map/all_to_all | solution.py:209
  30.0 0.2 reshape.89
  30.2 5.4 %gather_fusion = f32[1024,1024]{1,0:T(8,128)} fusion(f32[64,1024]{1,0:T(8,128)S(1)} %reshape.89, s32[1024]{0:T(1024)S(1)} %fusion.3), kind=kCustom, calls=%fused_computation | custom fusion | bytes 8392704 | tf_op jit(solution)/shard_map/jit(_take)/gather | solution.py:216
  35.7 5.6 %add_convert_fusion.mk_ref = bf16[1024,1024]{1,0:T(8,128)(2,1)} fusion(f32[1024,1024]{1,0:T(8,128)} %param.13, f32[1024,1024]{1,0:T(8,128)} %gather_fusion, pred[1024]{0:T(1024)(128)(4,1)S(1)} %compare_and_fusion), kind=kLoop, calls=%fused_computation.5 | loop fusion | flops 4194304 | bytes 10486784 | tf_op jit(solution)/shard_map/convert_element_type | solution.py:216
  41.2 85.8 %all-gather.3.cloned.1.call-done.rest_0_.rest_1_.rest_2_.rest_3_.rest_4_.rest_5_.rest_6_.rest_7_.rest_8_.rest_9_.rest_10_.rest_11_.rest_12_.rest_13_.rest_14_.rest_15_ = bf16[8192,2048]{1,0:T(8,128)(2,1)} async-done(((bf16[256,2048]{1,0:T(8,128)(2,1)}), bf16[8192,2048]{1,0:T(8,128)(2,1)}) %all-gather.3.cloned.1.call-update) | async-done | bytes 33554448 | tf_op jit(solution)/shard_map/all_gather | solution.py:204
  127.0 30.6 %shard_map.128 = (bf16[256,1024]{1,0:T(8,128)(2,1)}, bf16[256,1024]{1,0:T(8,128)(2,1)}, f32[2,1024,1024]{2,1,0:T(8,128)}, f32[24,256]{1,0:T(8,128)}) custom-call(s32[2]{0:T(128)} %dynamic_slice.12.cnt_ref, s32[16]{0:T(128)} %reshape.88.nb_ref, bf16[256,1024]{1,0:T(8,128)(2,1)} %bitcast.24, bf16[256,1024]{1,0:T(8,128)(2,1)} %bitcast.26, ...), custom_call_target="tpu_custom_call" | custom-call | flops 5905580032 | bytes 23068672 | tf_op jit(solution)/shard_map/pallas_call | solution.py:97
  157.6 1.7 broadcast_in_dim.76
  159.3 5.2 %all-to-all-start.1 = ((f32[32,24,256]{2,1,0:T(8,128)}), f32[32,24,256]{2,1,0:T(8,128)S(1)}, u32[]{:S(2)}, u32[]{:S(2)}) async-start(f32[32,24,256]{2,1,0:T(8,128)} %broadcast_in_dim.76), calls=%async_computation.1 | async-start | bytes 1572864 | tf_op jit(solution)/shard_map/all_to_all | solution.py:228
  164.5 6.3 %reduce_sum.75 = bf16[1024,1024]{1,0:T(8,128)(2,1)} reduce(f32[2,1024,1024]{2,1,0:T(8,128)} %get-tuple-element.19, f32[]{:T(128)} %constant.30.clone.1), dimensions={0}, to_apply=%region_8.9 | reduce | flops 1048576 | bytes 10485764 | tf_op jit(solution)/shard_map/reduce_sum | solution.py:235
  170.8 76.8 %all-gather.5.cloned.1.call-done.qd_ref = bf16[8192,2048]{1,0:T(8,128)(2,1)} async-done(((bf16[256,2048]{1,0:T(8,128)(2,1)}), bf16[8192,2048]{1,0:T(8,128)(2,1)}) %all-gather.5.cloned.1.call-update) | async-done | bytes 33554448 | tf_op jit(solution)/shard_map/all_gather | solution.py:222
  247.6 5.0 %all-to-all-start.2 = ((bf16[32,32,1024]{2,1,0:T(8,128)(2,1)}), bf16[32,32,1024]{2,1,0:T(8,128)(2,1)S(1)}, u32[]{:S(2)}, u32[]{:S(2)}) async-start(bf16[32,32,1024]{2,1,0:T(8,128)(2,1)} %bitcast.17), calls=%async_computation.2 | async-start | bytes 4194304 | tf_op jit(solution)/shard_map/all_to_all | solution.py:236
  252.6 0.1 copy.18
  252.7 0.1 reduce_or.14
  252.9 0.1 reduce_or.18
  253.0 0.6 convert_reduce_fusion.2
  254.3 0.1 eq.32
  254.4 1.6 sort.17
  256.0 0.6 dynamic_slice.14
  256.6 1.8 compare_select_fusion.1
  258.4 0.6 iota_reduce_fusion
  259.0 1.2 gather_fusion.1
  260.2 1.2 gather_fusion.2
  261.4 0.1 reduce_sum.73
  261.5 0.1 reduce_sum.74
  261.7 1.2 gather_fusion.3
  262.9 1.2 compare_convert_fusion.src_live
  264.1 0.8 dynamic-slice_subtract_fusion
  264.9 31.3 %shard_map.129 = (f32[256,1024]{1,0:T(8,128)}, f32[256,1024]{1,0:T(8,128)}) custom-call(s32[32]{0:T(128)} %gather_fusion.1, s32[32]{0:T(128)} %get-tuple-element.28.src_dev, s32[32]{0:T(128)} %gather_fusion.2, s32[32]{0:T(128)} %compare_convert_fusion.src_live, s32[32]{0:T(128)} %gather_fusion.3, bf16[8192,2048]{1,0:T(8,128)(2,1)} %all-gather.5.cloned.1.call-done.qd_ref, ...), custom_call_target="tpu_custom_call" | custom-call | flops 4294967296 | bytes 22020096 | tf_op jit(solution)/shard_map/pallas_call | solution.py:167
  296.2 0.4 convert_reduce_fusion
  296.6 0.8 broadcast_in_dim.80
  297.4 4.3 %all-to-all-start.3 = ((f32[4,32,1024]{2,1,0:T(8,128)}), f32[4,32,1024]{2,1,0:T(8,128)S(1)}, u32[]{:S(2)}, u32[]{:S(2)}) async-start(f32[4,32,1024]{2,1,0:T(8,128)} %broadcast_in_dim.80), calls=%async_computation.3 | async-start | bytes 1048576 | tf_op jit(solution)/shard_map/all_to_all | solution.py:269
  301.7 2.1 convert_bitcast_fusion
  303.8 0.1 select_reduce_fusion
  304.0 0.9 fusion
  304.8 5.0 %all-to-all-done.3 = f32[4,32,1024]{2,1,0:T(8,128)S(1)} async-done(((f32[4,32,1024]{2,1,0:T(8,128)}), f32[4,32,1024]{2,1,0:T(8,128)S(1)}, u32[]{:S(2)}, u32[]{:S(2)}) %all-to-all-start.3) | async-done | bytes 524320 | tf_op jit(solution)/shard_map/all_to_all | solution.py:269
  309.8 0.7 reduce_sum.78
  (32 shorter events, 0.2 us)
Async XLA Ops:
  7.2 4.8 %copy-start = (bf16[1,256,1024]{2,1,0:T(8,128)(2,1)S(1)}, bf16[1,256,1024]{2,1,0:T(8,128)(2,1)}, u32[]{:S(2)}) copy-start(bf16[1,256,1024]{2,1,0:T(8,128)(2,1)} %param.11) | copy-start | bytes 1572868
  7.2 14.0 %copy-start.3 = (s32[1024]{0:T(1024)S(1)}, s32[1024]{0:T(1024)}, u32[]{:S(2)}) copy-start(s32[1024]{0:T(1024)} %param.17) | copy-start | bytes 12292
  7.2 14.0 %copy-start.6 = (s32[64,8]{0,1:T(8,128)S(1)}, s32[64,8]{0,1:T(8,128)}, u32[]{:S(2)}) copy-start(s32[64,8]{0,1:T(8,128)} %param.14) | copy-start | bytes 6148
  7.2 14.0 %copy-start.5 = (s32[64,8]{0,1:T(8,128)S(1)}, s32[64,8]{0,1:T(8,128)}, u32[]{:S(2)}) copy-start(s32[64,8]{0,1:T(8,128)} %param.15) | copy-start | bytes 6148
  7.2 16.0 %copy-start.8 = (s32[64]{0:T(128)S(1)}, s32[64]{0:T(128)}, u32[]{:S(2)}) copy-start(s32[64]{0:T(128)} %param.16) | copy-start | bytes 772
  7.2 119.8 %all-gather.3.cloned.1.call-start = ((), (), s32[]{:S(2)}) async-start(), calls=%async_computation.4 | async-start | bytes 34603008 | tf_op jit(solution)/shard_map/all_gather | solution.py:204
  9.6 238.0 %all-gather.5.cloned.1.call-start = ((), (), s32[]{:S(2)}) async-start(), calls=%async_computation.5 | async-start | bytes 34603008 | tf_op jit(solution)/shard_map/all_gather | solution.py:222
  12.9 17.2 %all-to-all-start = ((f32[32,2,1024]{2,1,0:T(2,128)}), f32[32,2,1024]{2,1,0:T(2,128)S(1)}, u32[]{:S(2)}, u32[]{:S(2)}) async-start(f32[32,2,1024]{2,1,0:T(2,128)} %broadcast_in_dim.70), calls=%async_computation | async-start | bytes 524288 | tf_op jit(solution)/shard_map/all_to_all | solution.py:209
  159.3 88.3 %all-to-all-start.1 = ((f32[32,24,256]{2,1,0:T(8,128)}), f32[32,24,256]{2,1,0:T(8,128)S(1)}, u32[]{:S(2)}, u32[]{:S(2)}) async-start(f32[32,24,256]{2,1,0:T(8,128)} %broadcast_in_dim.76), calls=%async_computation.1 | async-start | bytes 1572864 | tf_op jit(solution)/shard_map/all_to_all | solution.py:228
  170.8 81.8 %copy-start.4 = (pred[64,8]{0,1:T(8,128)(4,1)S(1)}, pred[64,8]{0,1:T(8,128)(4,1)}, u32[]{:S(2)}) copy-start(pred[64,8]{0,1:T(8,128)(4,1)} %get-tuple-element.26) | copy-start | bytes 1540
  170.8 81.9 %copy-start.9 = (s32[64]{0:T(128)S(1)}, s32[64]{0:T(128)}, u32[]{:S(2)}) copy-start(s32[64]{0:T(128)} %param.16) | copy-start | bytes 772
  170.8 90.6 %copy-start.7 = (s32[64]{0:T(128)S(1)}, s32[64]{0:T(128)}, u32[]{:S(2)}) copy-start(s32[64]{0:T(128)} %get-tuple-element.25) | copy-start | bytes 772
  247.6 17.3 %copy-start.1 = (f32[32,24,256]{2,1,0:T(8,128)}, f32[32,24,256]{2,1,0:T(8,128)S(1)}, u32[]{:S(2)}) copy-start(f32[32,24,256]{2,1,0:T(8,128)S(1)} %all-to-all-done.1.st_ref) | copy-start | bytes 2359300
  247.6 48.6 %all-to-all-start.2 = ((bf16[32,32,1024]{2,1,0:T(8,128)(2,1)}), bf16[32,32,1024]{2,1,0:T(8,128)(2,1)S(1)}, u32[]{:S(2)}, u32[]{:S(2)}) async-start(bf16[32,32,1024]{2,1,0:T(8,128)(2,1)} %bitcast.17), calls=%async_computation.2 | async-start | bytes 4194304 | tf_op jit(solution)/shard_map/all_to_all | solution.py:236
  296.2 7.7 %copy-start.2 = (f32[256,1024]{1,0:T(8,128)S(1)}, f32[256,1024]{1,0:T(8,128)}, u32[]{:S(2)}) copy-start(f32[256,1024]{1,0:T(8,128)} %get-tuple-element.23) | copy-start | bytes 3145732
  297.4 12.4 %all-to-all-start.3 = ((f32[4,32,1024]{2,1,0:T(8,128)}), f32[4,32,1024]{2,1,0:T(8,128)S(1)}, u32[]{:S(2)}, u32[]{:S(2)}) async-start(f32[4,32,1024]{2,1,0:T(8,128)} %broadcast_in_dim.80), calls=%async_computation.3 | async-start | bytes 1048576 | tf_op jit(solution)/shard_map/all_to_all | solution.py:269
Sparse Core Ops, SparseCore 0:
  10.3 116.6 all-gather.2
  129.3 118.2 all-gather.4
where the time goes:
time: 322 us; the launch traced here: 317 us
  waiting for transfers between devices  174 us (54%)
  Pallas kernels  61.9 us (19%)
  other arithmetic  28.9 us (9%)
  starting transfers between devices  22.8 us (7%)
  local copies, waits for them, and re-layouts  15.1 us (5%)
  between operations  14.9 us (5%)
    all_gather x1, waiting for transfers between devices, shards(): lax.all_gather(jnp.concatenate([key_states[0], value_states[0]], axis=-1)...  85.8 us
    all_gather x1, waiting for transfers between devices, shards(): lax.all_gather(jnp.concatenate([queries[0], out_grad[0]], axis=-1), 'seq'...  76.8 us
    pallas_call x1, Pallas kernels, owner_core(): pl.pallas_call(_owner_body, grid_spec=grid_spec, out_shape=[jax.ShapeDtyp...  31.3 us
    pallas_call x1, Pallas kernels, query_core(): pl.pallas_call(_query_body, grid_spec=grid_spec, out_shape=[jax.ShapeDtyp...  30.6 us
    all_to_all x1, starting transfers between devices, shards(): lax.all_to_all(jnp.broadcast_to(value_sums[None], (seq_devices, local_blo...  8.27 us
  transfers between devices with their start and end apart: 6, of which 4 were waited for; matrix products, arithmetic and copies ran while one was open for 13% of the time, Pallas kernels for 20%

commit v1 on v0

--- a/solution.py
+++ b/solution.py
@@ -139,7 +139,7 @@
             row_total = st[heads + h : heads + h + 1]
             grad_dot = st[2 * heads + h : 2 * heads + h + 1]
             score_t = lax.dot_general(k_h, q_h, nt, preferred_element_type=f32) * scale
-            prob_t = jnp.exp(score_t - row_max) / row_total
+            prob_t = jnp.exp(score_t - row_max) * (1.0 / row_total)
             weight_t = prob_t.astype(jnp.bfloat16)
             dprob_t = lax.dot_general(v_h, do_h, nt, preferred_element_type=f32)
             dscore_t = (prob_t * (dprob_t - grad_dot)).astype(jnp.bfloat16)
@@ -222,25 +222,6 @@
     qd_all = lax.all_gather(
         jnp.concatenate([queries[0], out_grad[0]], axis=-1), "seq", axis=0, tiled=True
     )
-    attended_rows, query_rows_grad, term, stats = query_core(
-        my_count, my_near, queries[0], out_grad[0], memory_keys, kv_all
-    )
-    stats_all = lax.all_to_all(
-        jnp.broadcast_to(stats[None], (seq_devices,) + stats.shape),
-        "seq",
-        split_axis=0,
-        concat_axis=0,
-        tiled=True,
-    )
-    term_rows, qd_all = lax.optimization_barrier((jnp.sum(term, axis=0).astype(jnp.bfloat16), qd_all))
-    row_parts = lax.all_to_all(
-        term_rows.reshape(seq_devices, rows_dev, row_width),
-        "seq",
-        split_axis=0,
-        concat_axis=0,
-        tiled=True,
-    )
-    row_grads = jnp.sum(row_parts.astype(jnp.float32), axis=0)
     near_width = near_device.shape[1]
     entries = local_blocks * near_width
     target = near_device.reshape(seq_devices, entries)
@@ -260,6 +241,29 @@
     position = jnp.arange(seq_devices, dtype=jnp.int32)
     pick = jnp.where(position < live_count, order, order[jnp.maximum(live_count - 1, 0)])
     live_in_order = (position < live_count).astype(jnp.int32)
+    t_blk, t_slot, t_my = src_blk[pick], src_slot[pick], my_slot[pick]
+    pick, t_blk, t_slot, t_my, live_in_order, memory_keys = lax.optimization_barrier(
+        (pick, t_blk, t_slot, t_my, live_in_order, memory_keys)
+    )
+    attended_rows, query_rows_grad, term, stats = query_core(
+        my_count, my_near, queries[0], out_grad[0], memory_keys, kv_all
+    )
+    stats_all = lax.all_to_all(
+        jnp.broadcast_to(stats[None], (seq_devices,) + stats.shape),
+        "seq",
+        split_axis=0,
+        concat_axis=0,
+        tiled=True,
+    )
+    term_rows, qd_all = lax.optimization_barrier((jnp.sum(term, axis=0).astype(jnp.bfloat16), qd_all))
+    row_parts = lax.all_to_all(
+        term_rows.reshape(seq_devices, rows_dev, row_width),
+        "seq",
+        split_axis=0,
+        concat_axis=0,
+        tiled=True,
+    )
+    row_grads = jnp.sum(row_parts.astype(jnp.float32), axis=0)
     my_writers = (
         lax.dynamic_slice_in_dim(writer_block, my_index * rows_dev, rows_dev, 0)
         - my_index * local_blocks
@@ -275,7 +279,7 @@
     )
     memory_grad = jnp.sum(all_rows, axis=0)
     dk_sum, dv_sum = owner_core(
-        src_blk[pick], pick, src_slot[pick], live_in_order, my_slot[pick], qd_all, stats_all,
+        t_blk, pick, t_slot, live_in_order, t_my, qd_all, stats_all,
         key_states[0], value_states[0],
     )
     value_sum = dv_sum.reshape(local_blocks, BLK, row_width)

time: 322 us -> 313 us (0.972)
  the two profiles are of different devices: /device:TPU:0 before, /device:TPU:7 now
where the time goes in v1:
time: 313 us; the launch traced here: 312 us
  waiting for transfers between devices  162 us (52%)
  Pallas kernels  69.5 us (22%)
  other arithmetic  27.7 us (9%)
  starting transfers between devices  23.5 us (8%)
  local copies, waits for them, and re-layouts  15.1 us (5%)
  between operations  14.9 us (5%)
    all_gather x1, waiting for transfers between devices, shards(): lax.all_gather(jnp.concatenate([key_states[0], value_states[0]], axis=-1)...  81.5 us
    all_gather x1, waiting for transfers between devices, shards(): lax.all_gather(jnp.concatenate([queries[0], out_grad[0]], axis=-1), 'seq'...  76.4 us
    pallas_call x1, Pallas kernels, owner_core(): pl.pallas_call(_owner_body, grid_spec=grid_spec, out_shape=[jax.ShapeDtyp...  39 us
    pallas_call x1, Pallas kernels, query_core(): pl.pallas_call(_query_body, grid_spec=grid_spec, out_shape=[jax.ShapeDtyp...  30.6 us
    all_to_all x1, starting transfers between devices, shards(): lax.all_to_all(jnp.broadcast_to(value_sums[None], (seq_devices, local_blo...  8.69 us
    reduce_sum x1, other arithmetic, shards(): jnp.sum(term, axis=0).astype(jnp.bfloat16)  6.32 us
  transfers between devices with their start and end apart: 6, of which 3 were waited for; matrix products, arithmetic and copies ran while one was open for 12% of the time, Pallas kernels for 22%

profile of v1, /device:TPU:7, one launch (start us, length us, event | category | flops | bytes accessed | tf_op | source)
XLA Modules:
  0.0 312.4 jit_solution(12997471862706748463)
XLA Ops:
  7.2 0.0 all-gather.3.cloned.1.call-start
  7.3 2.3 pad_maximum_fusion
  9.6 0.0 all-gather.3.cloned.1.call-update
  9.6 0.0 all-gather.5.cloned.1.call-start
  9.7 2.3 pad_maximum_fusion.1
  12.0 0.0 all-gather.5.cloned.1.call-update
  12.0 0.1 convert_reduce_fusion.1
  12.1 0.8 broadcast_in_dim.73
  12.9 8.7 %all-to-all-start = ((f32[32,2,1024]{2,1,0:T(2,128)}), f32[32,2,1024]{2,1,0:T(2,128)S(1)}, u32[]{:S(2)}, u32[]{:S(2)}) async-start(f32[32,2,1024]{2,1,0:T(2,128)} %broadcast_in_dim.73), calls=%async_computation | async-start | bytes 524288 | tf_op jit(solution)/shard_map/all_to_all | solution.py:209
  21.6 0.1 copy.18
  21.7 0.1 reduce_or.14
  21.9 0.1 eq.32
  21.9 0.1 reduce_or.18
  22.1 0.6 convert_reduce_fusion.2
  23.4 1.6 sort.17
  25.0 0.6 dynamic_slice.14
  25.6 1.9 compare_select_fusion.1
  27.5 0.1 constant_dynamic-slice_fusion
  27.5 0.6 iota_reduce_fusion
  28.2 1.2 compare_convert_fusion.src_live
  29.4 0.6 dynamic_slice.12.cnt_ref
  30.0 1.3 gather_fusion.1
  31.3 1.3 gather_fusion
  32.5 0.1 reduce_sum.72
  32.6 0.1 reduce_sum.73
  32.8 1.2 gather_fusion.2
  34.0 0.1 copy.17
  34.1 0.6 reshape.88.nb_ref
  34.7 0.2 reshape.89
  34.9 5.4 %gather_fusion.3 = f32[1024,1024]{1,0:T(8,128)} fusion(f32[64,1024]{1,0:T(8,128)S(1)} %reshape.89, s32[1024]{0:T(1024)S(1)} %fusion.3), kind=kCustom, calls=%fused_computation.3 | custom fusion | bytes 8392704 | tf_op jit(solution)/shard_map/jit(_take)/gather | solution.py:216
  40.3 5.4 %add_convert_fusion.mk_ref = bf16[1024,1024]{1,0:T(8,128)(2,1)} fusion(f32[1024,1024]{1,0:T(8,128)} %param.13, f32[1024,1024]{1,0:T(8,128)} %gather_fusion.3, pred[1024]{0:T(1024)(128)(4,1)S(1)} %compare_and_fusion), kind=kLoop, calls=%fused_computation.5 | loop fusion | flops 4194304 | bytes 10486784 | tf_op jit(solution)/shard_map/convert_element_type | solution.py:216
  45.8 81.5 %all-gather.3.cloned.1.call-done.rest_0_.rest_1_.rest_2_.rest_3_.rest_4_.rest_5_.rest_6_.rest_7_.rest_8_.rest_9_.rest_10_.rest_11_.rest_12_.rest_13_.rest_14_.rest_15_ = bf16[8192,2048]{1,0:T(8,128)(2,1)} async-done(((bf16[256,2048]{1,0:T(8,128)(2,1)}), bf16[8192,2048]{1,0:T(8,128)(2,1)}) %all-gather.3.cloned.1.call-update) | async-done | bytes 33554448 | tf_op jit(solution)/shard_map/all_gather | solution.py:204
  127.3 30.6 %shard_map.128 = (bf16[256,1024]{1,0:T(8,128)(2,1)}, bf16[256,1024]{1,0:T(8,128)(2,1)}, f32[2,1024,1024]{2,1,0:T(8,128)}, f32[24,256]{1,0:T(8,128)}) custom-call(s32[2]{0:T(128)} %dynamic_slice.12.cnt_ref, s32[16]{0:T(128)} %reshape.88.nb_ref, bf16[256,1024]{1,0:T(8,128)(2,1)} %bitcast.24, bf16[256,1024]{1,0:T(8,128)(2,1)} %bitcast.26, ...), custom_call_target="tpu_custom_call" | custom-call | flops 5905580032 | bytes 23068672 | tf_op jit(solution)/shard_map/pallas_call | solution.py:97
  157.8 1.7 broadcast_in_dim.76
  159.5 5.4 %all-to-all-start.1 = ((f32[32,24,256]{2,1,0:T(8,128)}), f32[32,24,256]{2,1,0:T(8,128)S(1)}, u32[]{:S(2)}, u32[]{:S(2)}) async-start(f32[32,24,256]{2,1,0:T(8,128)} %broadcast_in_dim.76), calls=%async_computation.1 | async-start | bytes 1572864 | tf_op jit(solution)/shard_map/all_to_all | solution.py:251
  164.9 6.3 %reduce_sum.75 = bf16[1024,1024]{1,0:T(8,128)(2,1)} reduce(f32[2,1024,1024]{2,1,0:T(8,128)} %get-tuple-element.31, f32[]{:T(128)} %constant.58.clone.1), dimensions={0}, to_apply=%region_8.9 | reduce | flops 1048576 | bytes 10485764 | tf_op jit(solution)/shard_map/reduce_sum | solution.py:258
  171.2 76.4 %all-gather.5.cloned.1.call-done.qd_ref = bf16[8192,2048]{1,0:T(8,128)(2,1)} async-done(((bf16[256,2048]{1,0:T(8,128)(2,1)}), bf16[8192,2048]{1,0:T(8,128)(2,1)}) %all-gather.5.cloned.1.call-update) | async-done | bytes 33554448 | tf_op jit(solution)/shard_map/all_gather | solution.py:222
  247.7 5.3 %all-to-all-start.2 = ((bf16[32,32,1024]{2,1,0:T(8,128)(2,1)}), bf16[32,32,1024]{2,1,0:T(8,128)(2,1)S(1)}, u32[]{:S(2)}, u32[]{:S(2)}) async-start(bf16[32,32,1024]{2,1,0:T(8,128)(2,1)} %bitcast.17), calls=%async_computation.2 | async-start | bytes 4194304 | tf_op jit(solution)/shard_map/all_to_all | solution.py:259
  253.0 0.8 dynamic-slice_subtract_fusion
  253.8 39.0 %shard_map.129 = (f32[256,1024]{1,0:T(8,128)}, f32[256,1024]{1,0:T(8,128)}) custom-call(s32[32]{0:T(128)} %gather_fusion, s32[32]{0:T(128)} %get-tuple-element.27.src_dev, s32[32]{0:T(128)} %gather_fusion.1, s32[32]{0:T(128)} %compare_convert_fusion.src_live, s32[32]{0:T(128)} %gather_fusion.2, bf16[8192,2048]{1,0:T(8,128)(2,1)} %all-gather.5.cloned.1.call-done.qd_ref, ...), custom_call_target="tpu_custom_call" | custom-call | flops 4294967296 | bytes 22020096 | tf_op jit(solution)/shard_map/pallas_call | solution.py:167
  292.8 0.4 convert_reduce_fusion
  293.1 0.8 broadcast_in_dim.80
  294.0 4.0 %all-to-all-start.3 = ((f32[4,32,1024]{2,1,0:T(8,128)}), f32[4,32,1024]{2,1,0:T(8,128)S(1)}, u32[]{:S(2)}, u32[]{:S(2)}) async-start(f32[4,32,1024]{2,1,0:T(8,128)} %broadcast_in_dim.80), calls=%async_computation.3 | async-start | bytes 1048576 | tf_op jit(solution)/shard_map/all_to_all | solution.py:273
  298.0 2.1 convert_bitcast_fusion
  300.1 0.1 select_reduce_fusion
  300.2 0.9 fusion
  301.1 3.8 %all-to-all-done.3 = f32[4,32,1024]{2,1,0:T(8,128)S(1)} async-done(((f32[4,32,1024]{2,1,0:T(8,128)}), f32[4,32,1024]{2,1,0:T(8,128)S(1)}, u32[]{:S(2)}, u32[]{:S(2)}) %all-to-all-start.3) | async-done | bytes 524320 | tf_op jit(solution)/shard_map/all_to_all | solution.py:273
  304.9 0.7 reduce_sum.78
  (26 shorter events, 0.1 us)
Async XLA Ops:
  7.2 4.8 %copy-start = (bf16[1,256,1024]{2,1,0:T(8,128)(2,1)S(1)}, bf16[1,256,1024]{2,1,0:T(8,128)(2,1)}, u32[]{:S(2)}) copy-start(bf16[1,256,1024]{2,1,0:T(8,128)(2,1)} %param.11) | copy-start | bytes 1572868
  7.2 14.4 %copy-start.5 = (s32[64,8]{0,1:T(8,128)S(1)}, s32[64,8]{0,1:T(8,128)}, u32[]{:S(2)}) copy-start(s32[64,8]{0,1:T(8,128)} %param.14) | copy-start | bytes 6148
  7.2 14.4 %copy-start.4 = (s32[64,8]{0,1:T(8,128)S(1)}, s32[64,8]{0,1:T(8,128)}, u32[]{:S(2)}) copy-start(s32[64,8]{0,1:T(8,128)} %param.15) | copy-start | bytes 6148
  7.2 14.5 %copy-start.6 = (s32[64]{0:T(128)S(1)}, s32[64]{0:T(128)}, u32[]{:S(2)}) copy-start(s32[64]{0:T(128)} %param.16) | copy-start | bytes 772
  7.2 21.0 %copy-start.3 = (s32[1024]{0:T(1024)S(1)}, s32[1024]{0:T(1024)}, u32[]{:S(2)}) copy-start(s32[1024]{0:T(1024)} %param.17) | copy-start | bytes 12292
  7.2 120.1 %all-gather.3.cloned.1.call-start = ((), (), s32[]{:S(2)}) async-start(), calls=%async_computation.4 | async-start | bytes 34603008 | tf_op jit(solution)/shard_map/all_gather | solution.py:204
  9.6 238.0 %all-gather.5.cloned.1.call-start = ((), (), s32[]{:S(2)}) async-start(), calls=%async_computation.5 | async-start | bytes 34603008 | tf_op jit(solution)/shard_map/all_gather | solution.py:222
  12.9 21.9 %all-to-all-start = ((f32[32,2,1024]{2,1,0:T(2,128)}), f32[32,2,1024]{2,1,0:T(2,128)S(1)}, u32[]{:S(2)}, u32[]{:S(2)}) async-start(f32[32,2,1024]{2,1,0:T(2,128)} %broadcast_in_dim.73), calls=%async_computation | async-start | bytes 524288 | tf_op jit(solution)/shard_map/all_to_all | solution.py:209
  159.5 88.1 %all-to-all-start.1 = ((f32[32,24,256]{2,1,0:T(8,128)}), f32[32,24,256]{2,1,0:T(8,128)S(1)}, u32[]{:S(2)}, u32[]{:S(2)}) async-start(f32[32,24,256]{2,1,0:T(8,128)} %broadcast_in_dim.76), calls=%async_computation.1 | async-start | bytes 1572864 | tf_op jit(solution)/shard_map/all_to_all | solution.py:251
  247.7 6.1 %copy-start.1 = (f32[32,24,256]{2,1,0:T(8,128)}, f32[32,24,256]{2,1,0:T(8,128)S(1)}, u32[]{:S(2)}) copy-start(f32[32,24,256]{2,1,0:T(8,128)S(1)} %all-to-all-done.1.st_ref) | copy-start | bytes 2359300
  247.7 45.1 %all-to-all-start.2 = ((bf16[32,32,1024]{2,1,0:T(8,128)(2,1)}), bf16[32,32,1024]{2,1,0:T(8,128)(2,1)S(1)}, u32[]{:S(2)}, u32[]{:S(2)}) async-start(bf16[32,32,1024]{2,1,0:T(8,128)(2,1)} %bitcast.17), calls=%async_computation.2 | async-start | bytes 4194304 | tf_op jit(solution)/shard_map/all_to_all | solution.py:259
  292.8 7.4 %copy-start.2 = (f32[256,1024]{1,0:T(8,128)S(1)}, f32[256,1024]{1,0:T(8,128)}, u32[]{:S(2)}) copy-start(f32[256,1024]{1,0:T(8,128)} %get-tuple-element.35) | copy-start | bytes 3145732
  294.0 10.9 %all-to-all-start.3 = ((f32[4,32,1024]{2,1,0:T(8,128)}), f32[4,32,1024]{2,1,0:T(8,128)S(1)}, u32[]{:S(2)}, u32[]{:S(2)}) async-start(f32[4,32,1024]{2,1,0:T(8,128)} %broadcast_in_dim.80), calls=%async_computation.3 | async-start | bytes 1048576 | tf_op jit(solution)/shard_map/all_to_all | solution.py:273
Sparse Core Ops, SparseCore 0:
  10.3 116.9 all-gather.2
  129.5 118.0 all-gather.4
